TPU v7x, 32 devices: a whole 2x2x4 slice. The times are simulated.
32 devices in a mesh: gx: 16 (over z, y, core), gy: 2 (over x).
Axes of the slice: x: 2, y: 2, z: 4, core: 2. Of those that a mesh axis runs over, the one named last changes fastest.
Arguments:
- field: float32 [6, 16, 256, 256], P(None, None, 'gx', 'gy'), may hold values from -6 to 6
- driver: float32 [6, 16, 256, 256], P(None, None, 'gx', 'gy'), may hold values from -6 to 6
- east_wind: float32 [16, 256, 256], P(None, 'gx', 'gy'), may hold values from -0.4 to 0.4
- north_wind: float32 [16, 256, 256], P(None, 'gx', 'gy'), may hold values from -0.4 to 0.4
Outputs:
- advected: float32 [6, 16, 256, 256], P(None, None, 'gx', 'gy')
- coeffs: float32 [6, 16, 4096], replicated
All inputs are finite; a program needn't handle non-finite values.
Results may differ from a plain program's by a relative error of at most 0.000098.
Values sent between devices are 32-bit elements; how exact they have to be, the bound alone decides.
A program may use at most 128 MiB of HBM per device.

v0:
```python
import math
import jax
import jax.numpy as jnp
from jax import lax
from jax.sharding import PartitionSpec as P

MX = 64
MY = 64


def shifted(value, axis, steps):
    count = lax.axis_size(axis)
    first, last = (max(0, -steps), min(count, count - steps))
    return lax.ppermute(value, axis, [(source, source + steps) for source in range(first, last)])


def padded(x, sides, width):
    for axis, dim in sides:
        peers, length = (lax.axis_size(axis), x.shape[dim])
        up = [(i, (i + 1) % peers) for i in range(peers - 1)]
        down = [(j, i) for i, j in up]
        last = lax.slice_in_dim(x, length - width, length, axis=dim)
        first = lax.slice_in_dim(x, 0, width, axis=dim)
        before = lax.ppermute(last, axis, up)
        after = lax.ppermute(first, axis, down)
        x = jnp.concatenate([before, x, after], axis=dim)
    return x


def cosine_table(first, count, total, modes):
    indices = first + jnp.arange(count, dtype=jnp.int32)
    wavenum = jnp.arange(modes, dtype=jnp.int32)
    phases = (wavenum[None, :] * (2 * indices[:, None] + 1)).astype(jnp.float32)
    cosines = jnp.cos(phases * (math.pi / (2.0 * total)))
    weight = jnp.where(wavenum == 0, math.sqrt(1.0 / total), math.sqrt(2.0 / total)).astype(
        jnp.float32
    )
    return cosines * weight[None, :]


def upwind(tracer, winds):
    east = winds[0]
    north = winds[1]
    east_flux = (
        jnp.maximum(east[:, :-1, :], 0.0) * tracer[..., :-1, :]
        + jnp.minimum(east[:, :-1, :], 0.0) * tracer[..., 1:, :]
    )
    north_flux = (
        jnp.maximum(north[:, :, :-1], 0.0) * tracer[..., :, :-1]
        + jnp.minimum(north[:, :, :-1], 0.0) * tracer[..., :, 1:]
    )
    inner = tracer[..., 1:-1, 1:-1]
    inner = inner - (east_flux[..., 1:, 1:-1] - east_flux[..., :-1, 1:-1])
    return inner - (north_flux[..., 1:-1, 1:] - north_flux[..., 1:-1, :-1])


def shards(field, driver, east_wind, north_wind):
    high = lax.Precision.HIGHEST
    tracers, levels, strip_cols, band_rows = field.shape
    nx_total = strip_cols * lax.axis_size("gx")
    ny_total = band_rows * lax.axis_size("gy")
    x_first = lax.axis_index("gx") * strip_cols
    y_first = lax.axis_index("gy") * band_rows
    x_table = cosine_table(x_first, strip_cols, nx_total, MX)
    y_table = cosine_table(y_first, band_rows, ny_total, MY)
    departure = driver - field
    half_proj = jnp.einsum("tlxy,xm->tlmy", departure, x_table, precision=high)
    partial_modes = jnp.einsum("tlmy,yn->tlmn", half_proj, y_table, precision=high)
    partial_modes = partial_modes.reshape(tracers, levels, MX * MY)
    coeffs = lax.psum(partial_modes, ("gx", "gy"))
    modal = coeffs.reshape(tracers, levels, MX, MY)
    large_scale = jnp.einsum("tlmn,yn->tlmy", modal, y_table, precision=high)
    large_scale = jnp.einsum("tlmy,xm->tlxy", large_scale, x_table, precision=high)
    nudged = field + 0.5 * large_scale
    xpos = x_first + jnp.arange(strip_cols, dtype=jnp.int32)
    ypos = y_first + jnp.arange(band_rows, dtype=jnp.int32)
    east_face = jnp.where(xpos[None, :, None] == nx_total - 1, jnp.float32(0.0), east_wind)
    north_face = jnp.where(ypos[None, None, :] == ny_total - 1, jnp.float32(0.0), north_wind)
    east_below = shifted(east_face[:, -1:, :], "gx", 1)
    north_below = shifted(north_face[:, :, -1:], "gy", 1)
    east_ext = jnp.concatenate([east_below, east_face, jnp.zeros_like(east_below)], axis=1)
    east_ext = jnp.pad(east_ext, ((0, 0), (0, 0), (1, 1)))
    north_ext = jnp.concatenate([north_below, north_face, jnp.zeros_like(north_below)], axis=2)
    north_ext = jnp.pad(north_ext, ((0, 0), (1, 1), (0, 0)))
    wind_ext = jnp.stack([east_ext, north_ext])
    advected = nudged
    for sweep in range(2):
        field_ext = padded(advected, (("gx", 2), ("gy", 3)), 1)
        advected = upwind(field_ext, wind_ext)
    return (advected, coeffs)


def solution(mesh):
    placed = (
        P(None, None, "gx", "gy"),
        P(None, None, "gx", "gy"),
        P(None, "gx", "gy"),
        P(None, "gx", "gy"),
    )
    return jax.shard_map(
        shards,
        mesh=mesh,
        in_specs=placed,
        out_specs=(P(None, None, "gx", "gy"), P()),
        check_vma=False,
    )
```

profile of v0, /device:TPU:8, one launch (start us, length us, event | category | flops | bytes accessed | tf_op | source)
XLA Modules:
  0.0 223.3 jit_solution(13646085363777777054)
XLA Ops:
  7.2 0.0 all-reduce.4.cloned.1.call-start
  7.3 0.5 copy-done.19
  7.8 4.2 %fusion.12 = f32[64,6,16,128]{3,0,2,1:T(8,128)S(1)} fusion(f32[6,16,16,128]{3,2,1,0:T(8,128)} %param.5, f32[6,16,16,128]{3,2,1,0:T(8,128)} %param.4, f32[64]{0:T(128)S(1)} %compare_select_fusion, s32[16]{0:T(128)S(1)} %multiply_add_fusion.1), kind=kOutput, calls=%fused_computation.29 | convolution fusion | flops 151195648 | bytes 4718912 | tf_op jit(solution)/shard_map/tlxy,xm->tlmy/dot_general | solution.py:67
  12.0 2.7 %fusion = f32[6,16,64,64]{3,2,1,0:T(8,128)S(1)} fusion(f32[64,6,16,128]{3,0,2,1:T(8,128)S(1)} %fusion.12, f32[64]{0:T(128)S(1)} %compare_select_fusion, s32[128]{0:T(128)S(1)} %multiply_add_fusion), kind=kOutput, calls=%fused_computation | convolution fusion | flops 604012544 | bytes 4719360 | tf_op jit(solution)/shard_map/tlmy,yn->tlmn/dot_general | solution.py:68
  14.7 0.0 copy-start.15
  14.7 0.0 copy-start.16
  14.7 1.9 reshape.47
  16.6 0.0 all-reduce.4.cloned.1.call-update
  16.7 0.1 slice.119
  16.8 3.4 %collective-permute-start.5 = (f32[16,16,1]{2,1,0:T(8,128)S(1)}, f32[16,16,1]{2,1,0:T(8,128)S(1)}, u32[]{:S(2)}, u32[]{:S(2)}) collective-permute-start(f32[16,16,1]{2,1,0:T(8,128)S(1)} %slice.119), channel_id=1, source_target_pairs={{0,1},{2,3},{4,5},{6,7},{8,9},{10,11},{12,13},{14,15},{16,17},{18,... | collective-permute-start | bytes 3080 | tf_op jit(solution)/shard_map/ppermute | solution.py:14
  20.2 0.1 broadcast_select_fusion.1
  20.3 2.1 collective-permute-start
  22.5 0.1 pad.36.clone
  22.5 0.7 pad.47.clone
  23.2 0.1 maximum_maximum_fusion
  23.3 0.8 fusion.17
  24.1 125.8 %all-reduce.4.cloned.1.call-done = f32[6,16,4096]{2,1,0:T(8,128)} async-done(((f32[6,16,4096]{2,1,0:T(8,128)}), f32[6,16,4096]{2,1,0:T(8,128)}) %all-reduce.4.cloned.1.call-update) | async-done | bytes 1572880 | tf_op jit(solution)/shard_map/psum | solution.py:70
  149.9 2.4 %reshape.48 = f32[6,16,64,64]{3,2,1,0:T(8,128)S(1)} reshape(f32[6,16,4096]{2,1,0:T(8,128)} %all-reduce.4.cloned.1.call-done) | data formatting | bytes 3145728 | tf_op jit(solution)/shard_map/reshape | solution.py:71
  152.3 0.0 copy-start.8
  152.3 3.6 %fusion.18 = f32[6,16,64,128]{3,2,1,0:T(8,128)S(1)} fusion(f32[6,16,64,64]{3,2,1,0:T(8,128)S(1)} %reshape.48, f32[64]{0:T(128)} %copy-done.17, s32[128]{0:T(128)} %copy-done.21), kind=kOutput, calls=%fused_computation.41 | convolution fusion | flops 604012544 | bytes 4719360 | tf_op jit(solution)/shard_map/tlmn,yn->tlmy/dot_general | solution.py:72
  156.0 1.7 fusion.7
  157.7 0.1 fusion.44
  157.7 1.9 collective-permute-start.2
  159.7 2.4 %collective-permute-start.1 = (f32[6,16,1,128]{3,2,1,0:T(1,128)S(1)}, f32[6,16,1,128]{3,2,1,0:T(1,128)S(1)}, u32[]{:S(2)}, u32[]{:S(2)}) collective-permute-start(f32[6,16,1,128]{3,2,1,0:T(1,128)S(1)} %get-tuple-element.8), channel_id=1, source_target_pairs={{0,2},{2,4},{4,6},{6,8},{8,10},{10,12},{12,14},{14,16},{16,18},{18... | collective-permute-start | bytes 147464 | tf_op jit(solution)/shard_map/ppermute | solution.py:24
  162.1 0.8 maximum_maximum_fusion.1
  162.9 3.1 %collective-permute-done.1 = f32[6,16,1,128]{3,2,1,0:T(1,128)S(1)} collective-permute-done((f32[6,16,1,128]{3,2,1,0:T(1,128)S(1)}, f32[6,16,1,128]{3,2,1,0:T(1,128)S(1)}, u32[]{:S(2)}, u32[]{:S(2)}) %collective-permute-start.1) | collective-permute-done | bytes 49184 | tf_op jit(solution)/shard_map/ppermute | solution.py:24
  166.0 0.2 pad_maximum_fusion.2
  166.2 0.4 fusion.42
  166.6 0.0 copy-done.13
  166.6 1.3 copy.6
  167.9 3.3 %collective-permute-start.3 = (f32[6,16,18,1]{2,1,3,0:T(8,128)}, f32[6,16,18,1]{2,1,3,0:T(8,128)S(1)}, u32[]{:S(2)}, u32[]{:S(2)}) collective-permute-start(f32[6,16,18,1]{2,1,3,0:T(8,128)} %copy.6), channel_id=1, source_target_pairs={{0,1},{2,3},{4,5},{6,7},{8,9},{10,11},{12,13},{14,15},{16,17},{18,... | collective-permute-start | bytes 20744 | tf_op jit(solution)/shard_map/ppermute | solution.py:24
  171.2 0.7 copy.7
  171.9 1.3 collective-permute-start.4
  173.1 2.2 fusion.15
  175.3 0.7 copy.8
  176.0 1.9 collective-permute-done.4
  177.9 1.5 copy.9
  179.4 2.3 %pad_maximum_fusion = f32[6,16,18,130]{3,2,1,0:T(8,128)S(1)} fusion(f32[6,16,18,1]{3,2,1,0:T(8,128)S(1)} %copy.9, f32[6,16,1,128]{3,2,1,0:T(1,128)} %copy-done.11, f32[6,16,16,128]{3,2,1,0:T(8,128)S(1)} %fusion.7, f32[6,16,1,128]{3,2,1,0:T(1,128)} %copy-done.13, f32[6,16,18,1]{3,2,1,0:T(8,128)S(1)} %copy.8), kind=kLoop, calls=%fused_computation.8 | loop fusion | flops 898560 | bytes 1797120 | tf_op jit(solution)/shard_map/concatenate | solution.py:26
  181.8 0.4 fusion.3
  182.2 0.5 copy-done.2
  182.8 1.3 fusion.4
  184.0 0.7 fusion.10
  184.7 0.1 fusion.43
  184.8 1.9 collective-permute-start.7
  186.7 2.6 %collective-permute-start.6 = (f32[6,16,1,128]{3,2,1,0:T(1,128)S(1)}, f32[6,16,1,128]{3,2,1,0:T(1,128)S(1)}, u32[]{:S(2)}, u32[]{:S(2)}) collective-permute-start(f32[6,16,1,128]{3,2,1,0:T(1,128)S(1)} %get-tuple-element.6), channel_id=1, source_target_pairs={{0,2},{2,4},{4,6},{6,8},{8,10},{10,12},{12,14},{14,16},{16,18},{18... | collective-permute-start | bytes 147464 | tf_op jit(solution)/shard_map/ppermute | solution.py:24
  189.3 3.9 %collective-permute-done.6 = f32[6,16,1,128]{3,2,1,0:T(1,128)S(1)} collective-permute-done((f32[6,16,1,128]{3,2,1,0:T(1,128)S(1)}, f32[6,16,1,128]{3,2,1,0:T(1,128)S(1)}, u32[]{:S(2)}, u32[]{:S(2)}) %collective-permute-start.6) | collective-permute-done | bytes 49184 | tf_op jit(solution)/shard_map/ppermute | solution.py:24
  193.2 0.2 pad_maximum_fusion.3
  193.4 1.4 fusion.41
  194.8 1.9 copy.12
  196.7 3.2 %collective-permute-start.8 = (f32[6,16,18,1]{2,1,3,0:T(8,128)S(1)}, f32[6,16,18,1]{2,1,3,0:T(8,128)S(1)}, u32[]{:S(2)}, u32[]{:S(2)}) collective-permute-start(f32[6,16,18,1]{2,1,3,0:T(8,128)S(1)} %copy.12), channel_id=1, source_target_pairs={{0,1},{2,3},{4,5},{6,7},{8,9},{10,11},{12,13},{14,15},{16,17},{18,... | collective-permute-start | bytes 20744 | tf_op jit(solution)/shard_map/ppermute | solution.py:24
  200.0 0.7 copy.13
  200.7 1.3 collective-permute-start.9
  202.0 0.7 copy.14
  202.7 4.0 %collective-permute-done.9 = f32[6,16,18,1]{2,1,3,0:T(8,128)S(1)} collective-permute-done((f32[6,16,18,1]{2,1,3,0:T(8,128)S(1)}, f32[6,16,18,1]{2,1,3,0:T(8,128)S(1)}, u32[]{:S(2)}, u32[]{:S(2)}) %collective-permute-start.9) | collective-permute-done | bytes 6944 | tf_op jit(solution)/shard_map/ppermute | solution.py:25
  206.6 1.7 copy.15
  208.3 2.7 %pad_maximum_fusion.1 = f32[6,16,18,130]{3,2,1,0:T(8,128)S(1)} fusion(f32[6,16,18,1]{3,2,1,0:T(8,128)} %copy.15, f32[6,16,1,128]{3,2,1,0:T(1,128)S(1)} %collective-permute-done.7, f32[6,16,16,128]{3,2,1,0:T(8,128)S(1)} %fusion.10, f32[6,16,1,128]{3,2,1,0:T(1,128)S(1)} %collective-permute-done.6, f32[6,16,18,1]{3,2,1,0:T(8,128)S(1)} %copy.14), kind=kLoop, calls=%fused_computation.12 | loop fusion | flops 898560 | bytes 1797120 | tf_op jit(solution)/shard_map/concatenate | solution.py:26
  211.1 0.0 copy-start
  211.1 0.0 copy-start.3
  211.1 0.4 fusion.2
  211.6 0.8 copy-done
  212.4 0.1 copy-done.3
  212.4 1.3 fusion.5
  213.7 1.6 fusion.8
  215.3 1.1 copy.21
  (49 shorter events, 0.1 us)
Async XLA Ops:
  7.2 142.7 %all-reduce.4.cloned.1.call-start = ((), (), s32[]{:S(2)}) async-start(), calls=%async_computation | async-start | bytes 3145728 | tf_op jit(solution)/shard_map/psum | solution.py:70
  7.2 4.7 %copy-start.17 = (f32[64]{0:T(128)}, f32[64]{0:T(128)S(1)}, u32[]{:S(2)}) copy-start(f32[64]{0:T(128)S(1)} %compare_select_fusion) | copy-start | bytes 772
  7.2 0.5 copy-start.19
  7.8 4.2 %copy-start.21 = (s32[128]{0:T(128)}, s32[128]{0:T(128)S(1)}, u32[]{:S(2)}) copy-start(s32[128]{0:T(128)S(1)} %multiply_add_fusion) | copy-start | bytes 1540
  14.7 2.0 copy-start.15
  14.7 5.5 %copy-start.16 = (f32[16,16,128]{2,1,0:T(8,128)S(1)}, f32[16,16,128]{2,1,0:T(8,128)}, u32[]{:S(2)}) copy-start(f32[16,16,128]{2,1,0:T(8,128)} %param.6) | copy-start | bytes 393220
  16.8 6.4 %collective-permute-start.5 = (f32[16,16,1]{2,1,0:T(8,128)S(1)}, f32[16,16,1]{2,1,0:T(8,128)S(1)}, u32[]{:S(2)}, u32[]{:S(2)}) collective-permute-start(f32[16,16,1]{2,1,0:T(8,128)S(1)} %slice.119), channel_id=1, source_target_pairs={{0,1},{2,3},{4,5},{6,7},{8,9},{10,11},{12,13},{14,15},{16,17},{18,... | collective-permute-start | bytes 3080 | tf_op jit(solution)/shard_map/ppermute | solution.py:14
  20.3 2.9 %copy-start.9 = (f32[16,16,128]{2,1,0:T(8,128)}, f32[16,16,128]{2,1,0:T(8,128)S(1)}, u32[]{:S(2)}) copy-start(f32[16,16,128]{2,1,0:T(8,128)S(1)} %broadcast_select_fusion.1) | copy-start | bytes 393220
  20.3 141.7 %collective-permute-start = (f32[16,1,128]{2,1,0:T(1,128)S(1)}, f32[16,1,128]{2,1,0:T(1,128)S(1)}, u32[]{:S(2)}, u32[]{:S(2)}) collective-permute-start(f32[16,1,128]{2,1,0:T(1,128)S(1)} %slice.110), channel_id=1, source_target_pairs={{0,2},{2,4},{4,6},{6,8},{8,10},{10,12},{12,14},{14,16},{16,18},{18... | collective-permute-start | bytes 24584 | tf_op jit(solution)/shard_map/ppermute | solution.py:14
  152.3 3.6 %copy-start.8 = (f32[6,16,16,128]{3,2,1,0:T(8,128)S(1)}, f32[6,16,16,128]{3,2,1,0:T(8,128)}, u32[]{:S(2)}) copy-start(f32[6,16,16,128]{3,2,1,0:T(8,128)} %param.4) | copy-start | bytes 2359300
  152.3 3.6 %copy-start.18 = (f32[64]{0:T(128)S(1)}, f32[64]{0:T(128)}, u32[]{:S(2)}) copy-start(f32[64]{0:T(128)} %copy-done.17) | copy-start | bytes 772
  152.3 3.6 %copy-start.20 = (s32[16]{0:T(128)S(1)}, s32[16]{0:T(128)}, u32[]{:S(2)}) copy-start(s32[16]{0:T(128)} %copy-done.19) | copy-start | bytes 196
  155.9 6.1 %copy-start.10 = (f32[16,16,128]{2,1,0:T(8,128)S(1)}, f32[16,16,128]{2,1,0:T(8,128)}, u32[]{:S(2)}) copy-start(f32[16,16,128]{2,1,0:T(8,128)} %copy-done.9) | copy-start | bytes 393220
  156.0 6.1 %copy-start.22 = (f32[18]{0:T(128)S(1)}, f32[18]{0:T(128)}, u32[]{:S(2)}) copy-start(f32[18]{0:T(128)} %pad.47.clone) | copy-start | bytes 220
  157.7 5.1 %collective-permute-start.2 = (f32[6,16,1,128]{3,2,1,0:T(1,128)S(1)}, f32[6,16,1,128]{3,2,1,0:T(1,128)S(1)}, u32[]{:S(2)}, u32[]{:S(2)}) collective-permute-start(f32[6,16,1,128]{3,2,1,0:T(1,128)S(1)} %get-tuple-element.9), channel_id=1, source_target_pairs={{2,0},{4,2},{6,4},{8,6},{10,8},{12,10},{14,12},{16,14},{18,16},{20... | collective-permute-start | bytes 147464 | tf_op jit(solution)/shard_map/ppermute | solution.py:25
  159.7 6.3 %collective-permute-start.1 = (f32[6,16,1,128]{3,2,1,0:T(1,128)S(1)}, f32[6,16,1,128]{3,2,1,0:T(1,128)S(1)}, u32[]{:S(2)}, u32[]{:S(2)}) collective-permute-start(f32[6,16,1,128]{3,2,1,0:T(1,128)S(1)} %get-tuple-element.8), channel_id=1, source_target_pairs={{0,2},{2,4},{4,6},{6,8},{8,10},{10,12},{12,14},{14,16},{16,18},{18... | collective-permute-start | bytes 147464 | tf_op jit(solution)/shard_map/ppermute | solution.py:24
  162.9 3.7 %copy-start.11 = (f32[6,16,1,128]{3,2,1,0:T(1,128)}, f32[6,16,1,128]{3,2,1,0:T(1,128)S(1)}, u32[]{:S(2)}) copy-start(f32[6,16,1,128]{3,2,1,0:T(1,128)S(1)} %collective-permute-done.2) | copy-start | bytes 147460
  166.0 0.6 copy-start.13
  167.9 7.5 %collective-permute-start.3 = (f32[6,16,18,1]{2,1,3,0:T(8,128)}, f32[6,16,18,1]{2,1,3,0:T(8,128)S(1)}, u32[]{:S(2)}, u32[]{:S(2)}) collective-permute-start(f32[6,16,18,1]{2,1,3,0:T(8,128)} %copy.6), channel_id=1, source_target_pairs={{0,1},{2,3},{4,5},{6,7},{8,9},{10,11},{12,13},{14,15},{16,17},{18,... | collective-permute-start | bytes 20744 | tf_op jit(solution)/shard_map/ppermute | solution.py:24
  171.9 6.1 %collective-permute-start.4 = (f32[6,16,18,1]{2,1,3,0:T(8,128)S(1)}, f32[6,16,18,1]{2,1,3,0:T(8,128)}, u32[]{:S(2)}, u32[]{:S(2)}) collective-permute-start(f32[6,16,18,1]{2,1,3,0:T(8,128)S(1)} %copy.7), channel_id=1, source_target_pairs={{1,0},{3,2},{5,4},{7,6},{9,8},{11,10},{13,12},{15,14},{17,16},{19,... | collective-permute-start | bytes 20744 | tf_op jit(solution)/shard_map/ppermute | solution.py:25
  179.4 2.3 %copy-start.4 = (f32[16,17,130]{2,1,0:T(8,128)S(1)}, f32[16,17,130]{2,1,0:T(8,128)}, u32[]{:S(2)}) copy-start(f32[16,17,130]{2,1,0:T(8,128)} %get-tuple-element.12) | copy-start | bytes 424324
  179.4 2.3 %copy-start.6 = (f32[16,17,130]{2,1,0:T(8,128)S(1)}, f32[16,17,130]{2,1,0:T(8,128)}, u32[]{:S(2)}) copy-start(f32[16,17,130]{2,1,0:T(8,128)} %get-tuple-element.13) | copy-start | bytes 424324
  181.8 1.0 copy-start.2
  181.8 1.0 copy-start.12
  181.8 1.0 copy-start.14
  184.8 4.6 %collective-permute-start.7 = (f32[6,16,1,128]{3,2,1,0:T(1,128)S(1)}, f32[6,16,1,128]{3,2,1,0:T(1,128)S(1)}, u32[]{:S(2)}, u32[]{:S(2)}) collective-permute-start(f32[6,16,1,128]{3,2,1,0:T(1,128)S(1)} %get-tuple-element.7), channel_id=1, source_target_pairs={{2,0},{4,2},{6,4},{8,6},{10,8},{12,10},{14,12},{16,14},{18,16},{20... | collective-permute-start | bytes 147464 | tf_op jit(solution)/shard_map/ppermute | solution.py:25
  186.7 6.5 %collective-permute-start.6 = (f32[6,16,1,128]{3,2,1,0:T(1,128)S(1)}, f32[6,16,1,128]{3,2,1,0:T(1,128)S(1)}, u32[]{:S(2)}, u32[]{:S(2)}) collective-permute-start(f32[6,16,1,128]{3,2,1,0:T(1,128)S(1)} %get-tuple-element.6), channel_id=1, source_target_pairs={{0,2},{2,4},{4,6},{6,8},{8,10},{10,12},{12,14},{14,16},{16,18},{18... | collective-permute-start | bytes 147464 | tf_op jit(solution)/shard_map/ppermute | solution.py:24
  196.7 5.2 %collective-permute-start.8 = (f32[6,16,18,1]{2,1,3,0:T(8,128)S(1)}, f32[6,16,18,1]{2,1,3,0:T(8,128)S(1)}, u32[]{:S(2)}, u32[]{:S(2)}) collective-permute-start(f32[6,16,18,1]{2,1,3,0:T(8,128)S(1)} %copy.12), channel_id=1, source_target_pairs={{0,1},{2,3},{4,5},{6,7},{8,9},{10,11},{12,13},{14,15},{16,17},{18,... | collective-permute-start | bytes 20744 | tf_op jit(solution)/shard_map/ppermute | solution.py:24
  200.7 6.0 %collective-permute-start.9 = (f32[6,16,18,1]{2,1,3,0:T(8,128)S(1)}, f32[6,16,18,1]{2,1,3,0:T(8,128)S(1)}, u32[]{:S(2)}, u32[]{:S(2)}) collective-permute-start(f32[6,16,18,1]{2,1,3,0:T(8,128)S(1)} %copy.13), channel_id=1, source_target_pairs={{1,0},{3,2},{5,4},{7,6},{9,8},{11,10},{13,12},{15,14},{17,16},{19,... | collective-permute-start | bytes 20744 | tf_op jit(solution)/shard_map/ppermute | solution.py:25
  208.3 2.7 %copy-start.5 = (f32[16,17,130]{2,1,0:T(8,128)S(1)}, f32[16,17,130]{2,1,0:T(8,128)}, u32[]{:S(2)}) copy-start(f32[16,17,130]{2,1,0:T(8,128)} %get-tuple-element.12) | copy-start | bytes 424324
  208.3 2.8 %copy-start.7 = (f32[16,17,130]{2,1,0:T(8,128)S(1)}, f32[16,17,130]{2,1,0:T(8,128)}, u32[]{:S(2)}) copy-start(f32[16,17,130]{2,1,0:T(8,128)} %get-tuple-element.13) | copy-start | bytes 424324
  211.1 1.3 copy-start
  211.1 1.3 copy-start.3
  213.7 1.6 copy-start.1
Sparse Core Ops, SparseCore 0:
  16.8 133.0 all-reduce.3
where the time goes:
time: 224 us; the launch traced here: 223 us
  waiting for transfers between devices  139 us (62%)
  starting transfers between devices  23.5 us (10%)
  local copies, waits for them, and re-layouts  19.4 us (9%)
  other arithmetic  15 us (7%)
  between operations  14.6 us (7%)
  matrix products  12.1 us (5%)
    psum x1, waiting for transfers between devices, shards(): coeffs = lax.psum(partial_modes, ('gx', 'gy'))  126 us
    ppermute x4, starting transfers between devices, padded(): before = lax.ppermute(last, axis, up)  11.6 us
    ppermute x4, waiting for transfers between devices, padded(): before = lax.ppermute(last, axis, up)  6.99 us
    ppermute x4, starting transfers between devices, padded(): after = lax.ppermute(first, axis, down)  6.4 us
    ppermute x4, waiting for transfers between devices, padded(): after = lax.ppermute(first, axis, down)  5.89 us
    ppermute x2, starting transfers between devices, shifted(): lax.ppermute(value, axis, [(source, source + steps) for source in range(f...  5.5 us
    concatenate x4, other arithmetic, padded(): x = jnp.concatenate([before, x, after], axis=dim)  5.4 us
  transfers between devices with their start and end apart: 11, of which 5 were waited for; matrix products, arithmetic and copies ran while one was open for 7% of the time, Pallas kernels for 0%

commit v1 on v0

--- a/solution.py
+++ b/solution.py
@@ -67,7 +67,7 @@
     half_proj = jnp.einsum("tlxy,xm->tlmy", departure, x_table, precision=high)
     partial_modes = jnp.einsum("tlmy,yn->tlmn", half_proj, y_table, precision=high)
     partial_modes = partial_modes.reshape(tracers, levels, MX * MY)
-    coeffs = lax.psum(partial_modes, ("gx", "gy"))
+    coeffs = jnp.sum(lax.all_gather(partial_modes, ("gx", "gy")), axis=0)
     modal = coeffs.reshape(tracers, levels, MX, MY)
     large_scale = jnp.einsum("tlmn,yn->tlmy", modal, y_table, precision=high)
     large_scale = jnp.einsum("tlmy,xm->tlxy", large_scale, x_table, precision=high)

time: 224 us -> 384 us (1.71)
  waiting for transfers between devices: 139 us -> 276 us
  other arithmetic: 15 us -> 33.1 us
  starting transfers between devices: 23.5 us -> 27.8 us
    all_gather x0 -> x1, waiting for transfers between devices: none -> 268 us  [shards(): coeffs = jnp.sum(lax.all_gather(partial_modes, ('gx', 'gy')), axis=0)]
    psum x1 -> x0, waiting for transfers between devices: 126 us -> none  [shards(): coeffs = lax.psum(partial_modes, ('gx', 'gy'))]
    reduce_sum x0 -> x1, other arithmetic: none -> 18.1 us  [shards(): coeffs = jnp.sum(lax.all_gather(partial_modes, ('gx', 'gy')), axis=0)]
    ppermute x4, waiting for transfers between devices: 6.99 us -> 0.16 us  [padded(): before = lax.ppermute(last, axis, up)]
    ppermute x4, starting transfers between devices: 6.4 us -> 12.2 us  [padded(): after = lax.ppermute(first, axis, down)]
  transfers between devices with their start and end apart: 11 -> 11, of which waited for: 5 -> 6; matrix products, arithmetic and copies ran while one was open for 7% -> 9% of each run, Pallas kernels for 0% -> 0%
where the time goes in v1:
time: 384 us; the launch traced here: 383 us
  waiting for transfers between devices  276 us (72%)
  other arithmetic  33.1 us (9%)
  starting transfers between devices  27.8 us (7%)
  local copies, waits for them, and re-layouts  18.9 us (5%)
  between operations  14.5 us (4%)
  matrix products  12.2 us (3%)
    all_gather x1, waiting for transfers between devices, shards(): coeffs = jnp.sum(lax.all_gather(partial_modes, ('gx', 'gy')), axis=0)  268 us
    reduce_sum x1, other arithmetic, shards(): coeffs = jnp.sum(lax.all_gather(partial_modes, ('gx', 'gy')), axis=0)  18.1 us
    ppermute x4, starting transfers between devices, padded(): after = lax.ppermute(first, axis, down)  12.2 us
    ppermute x4, starting transfers between devices, padded(): before = lax.ppermute(last, axis, up)  10.1 us
    ppermute x4, waiting for transfers between devices, padded(): after = lax.ppermute(first, axis, down)  8.42 us
  transfers between devices with their start and end apart: 11, of which 6 were waited for; matrix products, arithmetic and copies ran while one was open for 9% of the time, Pallas kernels for 0%

profile of v1, /device:TPU:8, one launch (start us, length us, event | category | flops | bytes accessed | tf_op | source)
XLA Modules:
  0.0 382.7 jit_solution(10335583160947738923)
XLA Ops:
  7.2 0.0 all-gather.2.cloned.1.call-start
  7.3 0.5 copy-done.18
  7.8 4.2 %fusion.12 = f32[64,6,16,128]{3,0,2,1:T(8,128)S(1)} fusion(f32[6,16,16,128]{3,2,1,0:T(8,128)} %param.5, f32[6,16,16,128]{3,2,1,0:T(8,128)} %param.4, f32[64]{0:T(128)S(1)} %compare_select_fusion, s32[16]{0:T(128)S(1)} %multiply_add_fusion.1), kind=kOutput, calls=%fused_computation.29 | convolution fusion | flops 151195648 | bytes 4718912 | tf_op jit(solution)/shard_map/tlxy,xm->tlmy/dot_general | solution.py:67
  12.0 2.7 fusion
  14.7 0.0 copy-start.14
  14.7 0.0 copy-start.15
  14.7 1.9 all_gather_reshape.3
  16.7 0.0 all-gather.2.cloned.1.call-update
  16.7 0.1 slice.119
  16.8 3.4 collective-permute-start.5
  20.3 0.1 broadcast_select_fusion.1
  20.4 2.1 collective-permute-start
  22.5 0.7 pad.47.clone
  23.1 0.1 pad.36.clone
  23.2 0.1 maximum_maximum_fusion
  23.4 0.8 fusion.17
  24.2 267.5 %all-gather.2.cloned.1.call-done = f32[32,6,16,4096]{3,2,1,0:T(8,128)} async-done(((f32[1,6,16,4096]{3,2,1,0:T(8,128)}), f32[32,6,16,4096]{3,2,1,0:T(8,128)}) %all-gather.2.cloned.1.call-update) | async-done | bytes 50331664 | tf_op jit(solution)/shard_map/all_gather | solution.py:70
  291.7 18.1 %reduce_sum.9 = f32[6,16,4096]{2,1,0:T(8,128)} reduce(f32[32,6,16,4096]{3,2,1,0:T(8,128)} %all-gather.2.cloned.1.call-done, f32[]{:T(128)} %constant.4.clone.1), dimensions={0}, to_apply=%region_0.1 | reduce | flops 12189696 | bytes 51904516 | tf_op jit(solution)/shard_map/reduce_sum | solution.py:70
  309.8 2.4 reshape.44
  312.2 3.6 fusion.18
  315.9 1.7 fusion.7
  317.6 0.1 fusion.44
  317.7 2.2 collective-permute-start.1
  319.9 4.8 %collective-permute-start.2 = (f32[6,16,1,128]{3,2,1,0:T(1,128)S(1)}, f32[6,16,1,128]{3,2,1,0:T(1,128)S(1)}, u32[]{:S(2)}, u32[]{:S(2)}) collective-permute-start(f32[6,16,1,128]{3,2,1,0:T(1,128)S(1)} %get-tuple-element.9), channel_id=1, source_target_pairs={{2,0},{4,2},{6,4},{8,6},{10,8},{12,10},{14,12},{16,14},{18,16},{20... | collective-permute-start | bytes 147464 | tf_op jit(solution)/shard_map/ppermute | solution.py:25
  324.8 0.8 maximum_maximum_fusion.1
  325.5 0.9 collective-permute-done.2
  326.5 0.6 copy-done.12
  327.1 0.2 pad_maximum_fusion.2
  327.3 0.4 fusion.42
  327.6 1.3 copy.6
  328.9 2.8 collective-permute-start.3
  331.7 0.7 copy.7
  332.4 1.5 collective-permute-start.4
  333.9 2.2 fusion.15
  336.1 0.7 copy.8
  336.8 1.7 collective-permute-done.4
  338.5 1.5 copy.9
  340.0 2.3 pad_maximum_fusion
  342.3 0.0 copy-start.1
  342.3 0.4 fusion.3
  342.7 0.5 copy-done.1
  343.3 1.3 fusion.4
  344.5 0.7 fusion.10
  345.2 0.1 fusion.43
  345.3 1.9 collective-permute-start.6
  347.2 4.5 %collective-permute-start.7 = (f32[6,16,1,128]{3,2,1,0:T(1,128)S(1)}, f32[6,16,1,128]{3,2,1,0:T(1,128)S(1)}, u32[]{:S(2)}, u32[]{:S(2)}) collective-permute-start(f32[6,16,1,128]{3,2,1,0:T(1,128)S(1)} %get-tuple-element.7), channel_id=1, source_target_pairs={{2,0},{4,2},{6,4},{8,6},{10,8},{12,10},{14,12},{16,14},{18,16},{20... | collective-permute-start | bytes 147464 | tf_op jit(solution)/shard_map/ppermute | solution.py:25
  351.8 1.7 collective-permute-done.7
  353.5 0.2 pad_maximum_fusion.3
  353.7 1.4 fusion.41
  355.1 1.9 copy.12
  357.0 3.2 collective-permute-start.8
  360.3 0.7 copy.13
  361.0 1.3 collective-permute-start.9
  362.3 0.2 collective-permute-done.8
  362.4 0.7 copy.14
  363.1 4.1 %collective-permute-done.9 = f32[6,16,18,1]{2,1,3,0:T(8,128)S(1)} collective-permute-done((f32[6,16,18,1]{2,1,3,0:T(8,128)S(1)}, f32[6,16,18,1]{2,1,3,0:T(8,128)S(1)}, u32[]{:S(2)}, u32[]{:S(2)}) %collective-permute-start.9) | collective-permute-done | bytes 6944 | tf_op jit(solution)/shard_map/ppermute | solution.py:25
  367.2 1.7 copy.15
  368.9 2.7 pad_maximum_fusion.1
  371.7 0.0 copy-start.2
  371.7 0.4 fusion.2
  372.2 0.8 copy-done
  373.0 0.1 copy-done.2
  373.0 1.3 fusion.5
  374.3 1.6 fusion.8
  (47 shorter events, 0.1 us)
Async XLA Ops:
  7.2 284.5 %all-gather.2.cloned.1.call-start = ((), (), s32[]{:S(2)}) async-start(), calls=%async_computation | async-start | bytes 51904512 | tf_op jit(solution)/shard_map/all_gather | solution.py:70
  7.2 4.7 %copy-start.16 = (f32[64]{0:T(128)}, f32[64]{0:T(128)S(1)}, u32[]{:S(2)}) copy-start(f32[64]{0:T(128)S(1)} %compare_select_fusion) | copy-start | bytes 772
  7.2 0.5 copy-start.18
  7.8 4.2 %copy-start.20 = (s32[128]{0:T(128)}, s32[128]{0:T(128)S(1)}, u32[]{:S(2)}) copy-start(s32[128]{0:T(128)S(1)} %multiply_add_fusion) | copy-start | bytes 1540
  14.7 2.0 copy-start.14
  14.7 5.5 %copy-start.15 = (f32[16,16,128]{2,1,0:T(8,128)S(1)}, f32[16,16,128]{2,1,0:T(8,128)}, u32[]{:S(2)}) copy-start(f32[16,16,128]{2,1,0:T(8,128)} %param.6) | copy-start | bytes 393220
  16.8 6.4 %collective-permute-start.5 = (f32[16,16,1]{2,1,0:T(8,128)S(1)}, f32[16,16,1]{2,1,0:T(8,128)S(1)}, u32[]{:S(2)}, u32[]{:S(2)}) collective-permute-start(f32[16,16,1]{2,1,0:T(8,128)S(1)} %slice.119), channel_id=1, source_target_pairs={{0,1},{2,3},{4,5},{6,7},{8,9},{10,11},{12,13},{14,15},{16,17},{18,... | collective-permute-start | bytes 3080 | tf_op jit(solution)/shard_map/ppermute | solution.py:14
  20.3 2.9 copy-start.8
  20.4 304.4 %collective-permute-start = (f32[16,1,128]{2,1,0:T(1,128)S(1)}, f32[16,1,128]{2,1,0:T(1,128)S(1)}, u32[]{:S(2)}, u32[]{:S(2)}) collective-permute-start(f32[16,1,128]{2,1,0:T(1,128)S(1)} %slice.110), channel_id=1, source_target_pairs={{0,2},{2,4},{4,6},{6,8},{8,10},{10,12},{12,14},{14,16},{16,18},{18... | collective-permute-start | bytes 24584 | tf_op jit(solution)/shard_map/ppermute | solution.py:14
  312.2 3.7 copy-start.7
  312.2 3.7 copy-start.17
  312.2 3.7 copy-start.19
  315.9 8.8 %copy-start.9 = (f32[16,16,128]{2,1,0:T(8,128)S(1)}, f32[16,16,128]{2,1,0:T(8,128)}, u32[]{:S(2)}) copy-start(f32[16,16,128]{2,1,0:T(8,128)} %copy-done.8) | copy-start | bytes 393220
  315.9 8.8 %copy-start.21 = (f32[18]{0:T(128)S(1)}, f32[18]{0:T(128)}, u32[]{:S(2)}) copy-start(f32[18]{0:T(128)} %pad.47.clone) | copy-start | bytes 220
  317.7 7.8 %collective-permute-start.1 = (f32[6,16,1,128]{3,2,1,0:T(1,128)S(1)}, f32[6,16,1,128]{3,2,1,0:T(1,128)S(1)}, u32[]{:S(2)}, u32[]{:S(2)}) collective-permute-start(f32[6,16,1,128]{3,2,1,0:T(1,128)S(1)} %get-tuple-element.8), channel_id=1, source_target_pairs={{0,2},{2,4},{4,6},{6,8},{8,10},{10,12},{12,14},{14,16},{16,18},{18... | collective-permute-start | bytes 147464 | tf_op jit(solution)/shard_map/ppermute | solution.py:24
  319.9 6.6 %collective-permute-start.2 = (f32[6,16,1,128]{3,2,1,0:T(1,128)S(1)}, f32[6,16,1,128]{3,2,1,0:T(1,128)S(1)}, u32[]{:S(2)}, u32[]{:S(2)}) collective-permute-start(f32[6,16,1,128]{3,2,1,0:T(1,128)S(1)} %get-tuple-element.9), channel_id=1, source_target_pairs={{2,0},{4,2},{6,4},{8,6},{10,8},{12,10},{14,12},{16,14},{18,16},{20... | collective-permute-start | bytes 147464 | tf_op jit(solution)/shard_map/ppermute | solution.py:25
  325.5 0.9 copy-start.10
  326.5 0.6 copy-start.12
  328.9 7.1 %collective-permute-start.3 = (f32[6,16,18,1]{2,1,3,0:T(8,128)}, f32[6,16,18,1]{2,1,3,0:T(8,128)S(1)}, u32[]{:S(2)}, u32[]{:S(2)}) collective-permute-start(f32[6,16,18,1]{2,1,3,0:T(8,128)} %copy.6), channel_id=1, source_target_pairs={{0,1},{2,3},{4,5},{6,7},{8,9},{10,11},{12,13},{14,15},{16,17},{18,... | collective-permute-start | bytes 20744 | tf_op jit(solution)/shard_map/ppermute | solution.py:24
  332.4 6.1 %collective-permute-start.4 = (f32[6,16,18,1]{2,1,3,0:T(8,128)S(1)}, f32[6,16,18,1]{2,1,3,0:T(8,128)}, u32[]{:S(2)}, u32[]{:S(2)}) collective-permute-start(f32[6,16,18,1]{2,1,3,0:T(8,128)S(1)} %copy.7), channel_id=1, source_target_pairs={{1,0},{3,2},{5,4},{7,6},{9,8},{11,10},{13,12},{15,14},{17,16},{19,... | collective-permute-start | bytes 20744 | tf_op jit(solution)/shard_map/ppermute | solution.py:25
  339.9 2.3 copy-start.3
  339.9 2.3 copy-start.5
  342.3 1.0 copy-start.1
  342.3 1.0 copy-start.11
  342.3 1.0 copy-start.13
  345.3 6.5 %collective-permute-start.6 = (f32[6,16,1,128]{3,2,1,0:T(1,128)S(1)}, f32[6,16,1,128]{3,2,1,0:T(1,128)S(1)}, u32[]{:S(2)}, u32[]{:S(2)}) collective-permute-start(f32[6,16,1,128]{3,2,1,0:T(1,128)S(1)} %get-tuple-element.6), channel_id=1, source_target_pairs={{0,2},{2,4},{4,6},{6,8},{8,10},{10,12},{12,14},{14,16},{16,18},{18... | collective-permute-start | bytes 147464 | tf_op jit(solution)/shard_map/ppermute | solution.py:24
  347.2 6.3 %collective-permute-start.7 = (f32[6,16,1,128]{3,2,1,0:T(1,128)S(1)}, f32[6,16,1,128]{3,2,1,0:T(1,128)S(1)}, u32[]{:S(2)}, u32[]{:S(2)}) collective-permute-start(f32[6,16,1,128]{3,2,1,0:T(1,128)S(1)} %get-tuple-element.7), channel_id=1, source_target_pairs={{2,0},{4,2},{6,4},{8,6},{10,8},{12,10},{14,12},{16,14},{18,16},{20... | collective-permute-start | bytes 147464 | tf_op jit(solution)/shard_map/ppermute | solution.py:25
  357.0 5.4 %collective-permute-start.8 = (f32[6,16,18,1]{2,1,3,0:T(8,128)S(1)}, f32[6,16,18,1]{2,1,3,0:T(8,128)S(1)}, u32[]{:S(2)}, u32[]{:S(2)}) collective-permute-start(f32[6,16,18,1]{2,1,3,0:T(8,128)S(1)} %copy.12), channel_id=1, source_target_pairs={{0,1},{2,3},{4,5},{6,7},{8,9},{10,11},{12,13},{14,15},{16,17},{18,... | collective-permute-start | bytes 20744 | tf_op jit(solution)/shard_map/ppermute | solution.py:24
  361.0 6.2 %collective-permute-start.9 = (f32[6,16,18,1]{2,1,3,0:T(8,128)S(1)}, f32[6,16,18,1]{2,1,3,0:T(8,128)S(1)}, u32[]{:S(2)}, u32[]{:S(2)}) collective-permute-start(f32[6,16,18,1]{2,1,3,0:T(8,128)S(1)} %copy.13), channel_id=1, source_target_pairs={{1,0},{3,2},{5,4},{7,6},{9,8},{11,10},{13,12},{15,14},{17,16},{19,... | collective-permute-start | bytes 20744 | tf_op jit(solution)/shard_map/ppermute | solution.py:25
  368.9 2.7 copy-start.4
  368.9 2.8 copy-start.6
  371.7 1.3 copy-start
  371.7 1.3 copy-start.2
Sparse Core Ops, SparseCore 0:
  16.8 274.8 all-gather.1
